TPU v7x, 256 devices: a whole 4x4x8 slice. The times are simulated.
256 devices in a mesh: row: 16 (over z, core), col: 16 (over x, y).
Axes of the slice: x: 4, y: 4, z: 8, core: 2. Of those that a mesh axis runs over, the one named last changes fastest.
Arguments:
- tokens: bfloat16 [4096, 8192], P('row', 'col'), may hold values from -6 to 6
- out_grad: bfloat16 [4096, 8192], P('row', 'col'), may hold values from -1.5 to 1.5
- gate_weight: bfloat16 [112, 1024, 128], P('col', 'row'), may hold values from -0.1875 to 0.1875
- up_weight: bfloat16 [112, 1024, 128], P('col', 'row'), may hold values from -0.1875 to 0.1875
- down_weight: bfloat16 [112, 1024, 128], P('col', 'row'), may hold values from -0.125 to 0.125
- gate_rows: int32 [112, 8], P('col'), may hold values from 0 to 63, all different within a row
- up_rows: int32 [112, 8], P('col'), may hold values from 0 to 63, all different within a row
- down_columns: int32 [112, 8], P('col'), may hold values from 0 to 63, all different within a row
Outputs:
- output: bfloat16 [4096, 8192], P('row', 'col')
- input_grad: bfloat16 [4096, 8192], P('row', 'col')
- gate_weight_grad: bfloat16 [112, 1024, 128], P('col', 'row')
- up_weight_grad: bfloat16 [112, 1024, 128], P('col', 'row')
- down_weight_grad: bfloat16 [112, 1024, 128], P('col', 'row')
Inputs may be any that keep to these rules, and one draw needn't show every extreme that they name: `gate_rows`: each row names 8 different block-rows; every block-row is named in some row. `up_rows`: each row names 8 different block-rows; every block-row is named in some row. `down_columns`: each row names 8 different output block-columns; every block-column is named in some row.
All inputs are finite; a program needn't handle non-finite values.
Results may differ from a plain program's by a relative error of at most 0.018.
Values may be sent and summed in bfloat16 or wider, within the bound.
A program may use at most 128 MiB of HBM per device.

v0:
```python
import jax
import jax.numpy as jnp
from jax import lax
from jax.sharding import PartitionSpec as P

D = 8192
BS = 128
KG = 8
KH = 8
DB = 64


def spread(contrib, block_lists):
    rows_here = contrib.shape[0]
    zero_block = jnp.zeros((rows_here, DB, BS), jnp.float32)
    placed = zero_block.at[:, block_lists.reshape(-1)].add(contrib.reshape(rows_here, -1, BS))
    return placed.reshape(rows_here, D)


def shards(tokens, out_grad, gate_weight, up_weight, down_weight, gate_rows, up_rows, down_columns):
    panels = lax.all_gather(jnp.stack([tokens, out_grad]), "col", axis=2, tiled=True)
    panel_in, panel_grad = (panels[0], panels[1])
    rows_here = panel_in.shape[0]
    owned_slots = gate_weight.shape[0]
    tiles = lax.all_gather(
        jnp.concatenate([gate_weight, up_weight, down_weight], axis=0), "row", axis=1, tiled=True
    )
    gate_tiles = tiles[:owned_slots]
    up_tiles = tiles[owned_slots : 2 * owned_slots]
    down_tiles = tiles[2 * owned_slots :]
    gate_four = gate_tiles.reshape(owned_slots, KG, BS, BS)
    up_four = up_tiles.reshape(owned_slots, KG, BS, BS)
    blocks_in = panel_in.reshape(rows_here, DB, BS)
    picked_gate = jnp.take(blocks_in, gate_rows.reshape(-1), axis=1).reshape(
        rows_here, owned_slots, KG, BS
    )
    picked_up = jnp.take(blocks_in, up_rows.reshape(-1), axis=1).reshape(
        rows_here, owned_slots, KG, BS
    )
    gate_value = jnp.einsum(
        "tfkr,fkri->tfi", picked_gate, gate_four, preferred_element_type=jnp.float32
    )
    up_value = jnp.einsum("tfkr,fkri->tfi", picked_up, up_four, preferred_element_type=jnp.float32)
    sigmoid_gate = jax.nn.sigmoid(gate_value)
    silu_gate = gate_value * sigmoid_gate
    hidden = (silu_gate * up_value).astype(jnp.bfloat16)
    down_four = down_tiles.reshape(owned_slots, KH, BS, BS)
    out_part = jnp.einsum("tfi,fkji->tfkj", hidden, down_four, preferred_element_type=jnp.float32)
    partial_out = spread(out_part, down_columns)
    blocks_grad = panel_grad.reshape(rows_here, DB, BS)
    picked_grad = jnp.take(blocks_grad, down_columns.reshape(-1), axis=1).reshape(
        rows_here, owned_slots, KH, BS
    )
    hidden_grad = jnp.einsum(
        "tfkj,fkji->tfi", picked_grad, down_four, preferred_element_type=jnp.float32
    )
    gate_grad = (
        hidden_grad * up_value * sigmoid_gate * (1.0 + gate_value * (1.0 - sigmoid_gate))
    ).astype(jnp.bfloat16)
    up_grad = (hidden_grad * silu_gate).astype(jnp.bfloat16)
    from_gate = jnp.einsum(
        "tfi,fkri->tfkr", gate_grad, gate_four, preferred_element_type=jnp.float32
    )
    from_up = jnp.einsum("tfi,fkri->tfkr", up_grad, up_four, preferred_element_type=jnp.float32)
    partial_in = spread(from_gate, gate_rows) + spread(from_up, up_rows)
    gate_partial = jnp.einsum(
        "tfkr,tfi->fkri", picked_gate, gate_grad, preferred_element_type=jnp.float32
    ).reshape(owned_slots, KG * BS, BS)
    up_partial = jnp.einsum(
        "tfkr,tfi->fkri", picked_up, up_grad, preferred_element_type=jnp.float32
    ).reshape(owned_slots, KG * BS, BS)
    down_partial = jnp.einsum(
        "tfkj,tfi->fkji", picked_grad, hidden, preferred_element_type=jnp.float32
    ).reshape(owned_slots, KH * BS, BS)
    tile_sums = lax.psum_scatter(
        jnp.concatenate([gate_partial, up_partial, down_partial], axis=0).astype(jnp.bfloat16),
        "row",
        scatter_dimension=1,
        tiled=True,
    )
    panel_sums = lax.psum_scatter(
        jnp.stack([partial_out, partial_in]).astype(jnp.bfloat16),
        "col",
        scatter_dimension=2,
        tiled=True,
    )
    return (
        panel_sums[0],
        panel_sums[1],
        tile_sums[:owned_slots],
        tile_sums[owned_slots : 2 * owned_slots],
        tile_sums[2 * owned_slots :],
    )


def solution(mesh):
    in_specs = (
        P("row", "col"),
        P("row", "col"),
        P("col", "row", None),
        P("col", "row", None),
        P("col", "row", None),
        P("col", None),
        P("col", None),
        P("col", None),
    )
    out_specs = (
        P("row", "col"),
        P("row", "col"),
        P("col", "row", None),
        P("col", "row", None),
        P("col", "row", None),
    )
    return jax.shard_map(shards, mesh=mesh, in_specs=in_specs, out_specs=out_specs, check_vma=False)
```

profile of v0, /device:TPU:2, one launch (start us, length us, event | category | flops | bytes accessed | tf_op | source)
XLA Modules:
  0.0 436.0 jit_solution(9459463797062491396)
XLA Ops:
  7.2 1.8 pad_maximum_fusion.3
  9.1 1.1 copy.50
  10.2 1.1 copy.51
  11.3 0.8 pad_maximum_fusion.2
  12.2 0.8 reshape.183
  13.2 43.8 %all-gather.3.cloned.1.call-done = bf16[21,1024,128]{2,1,0:T(8,128)(2,1)} async-done(((bf16[21,64,128]{2,1,0:T(8,128)(2,1)}), bf16[21,1024,128]{2,1,0:T(8,128)(2,1)}) %all-gather.3.cloned.1.call-update) | async-done | bytes 5505040 | tf_op jit(solution)/shard_map/all_gather | solution.py:25
  57.1 4.9 %fusion.10 = (bf16[7,1024,128]{2,1,0:T(8,128)(2,1)}, bf16[7,1024,128]{2,1,0:T(8,128)(2,1)}, bf16[7,1024,128]{2,1,0:T(8,128)(2,1)S(1)}) fusion(bf16[21,1024,128]{2,1,0:T(8,128)(2,1)} %all-gather.3.cloned.1.call-done), kind=kLoop, calls=%fused_computation.48 | loop fusion | bytes 11010048 | tf_op jit(solution)/shard_map/slice | solution.py:29
  61.9 71.8 %all-gather.5.cloned.1.call-done = bf16[2,256,8192]{1,2,0:T(8,128)(2,1)} async-done(((bf16[2,256,512]{1,2,0:T(8,128)(2,1)}), bf16[2,256,8192]{1,2,0:T(8,128)(2,1)}) %all-gather.5.cloned.1.call-update) | async-done | bytes 8388624 | tf_op jit(solution)/shard_map/all_gather | solution.py:21
  133.7 5.7 %fusion.9 = (bf16[1,256,8192]{1,2,0:T(8,128)(2,1)}, bf16[1,256,8192]{1,2,0:T(8,128)(2,1)}) fusion(bf16[2,256,8192]{1,2,0:T(8,128)(2,1)} %all-gather.5.cloned.1.call-done), kind=kLoop, calls=%fused_computation.47 | loop fusion | bytes 16777216 | tf_op jit(solution)/shard_map/slice | solution.py:22
  139.4 6.4 %copy.52 = bf16[256,64,128]{2,0,1:T(8,128)(2,1)} copy(bf16[256,64,128]{0,2,1:T(8,128)(2,1)} %bitcast.106) | data formatting | bytes 8388608 | tf_op jit(solution)/shard_map/reshape;squeeze | solution.py:33
  145.9 6.4 %copy.59 = bf16[256,64,128]{2,0,1:T(8,128)(2,1)} copy(bf16[256,64,128]{0,2,1:T(8,128)(2,1)} %bitcast.105) | data formatting | bytes 8388608 | tf_op jit(solution)/shard_map/reshape;squeeze | solution.py:50
  152.2 5.1 %gather_fusion.1 = bf16[56,256,128]{2,1,0:T(8,128)(2,1)} fusion(bf16[256,64,128]{2,0,1:T(8,128)(2,1)} %copy.52, s32[1024]{0:T(1024)S(1)} %pad_clamp_fusion.1), kind=kCustom, calls=%fused_computation.1.clone | custom fusion | bytes 7340256 | tf_op jit(solution)/shard_map/jit(_take)/gather | solution.py:37
  157.3 5.1 %gather_fusion = bf16[56,256,128]{2,1,0:T(8,128)(2,1)} fusion(bf16[256,64,128]{2,0,1:T(8,128)(2,1)} %copy.52, s32[1024]{0:T(1024)S(1)} %pad_clamp_fusion.2), kind=kCustom, calls=%fused_computation.clone | custom fusion | bytes 7340256 | tf_op jit(solution)/shard_map/jit(_take)/gather | solution.py:34
  162.4 2.6 broadcast_select_fusion.1
  165.0 1.8 copy-done
  166.8 2.3 convolution_bitcast_fusion.1
  169.0 5.1 %gather_fusion.2 = bf16[56,256,128]{2,1,0:T(8,128)(2,1)} fusion(bf16[256,64,128]{2,0,1:T(8,128)(2,1)} %copy.59, s32[1024]{0:T(1024)S(1)} %pad_clamp_fusion), kind=kCustom, calls=%fused_computation.2.clone | custom fusion | bytes 7340256 | tf_op jit(solution)/shard_map/jit(_take)/gather | solution.py:51
  174.1 2.4 broadcast_select_fusion
  176.6 1.4 convolution_bitcast_fusion
  177.9 0.7 copy-done.3
  179.0 1.1 copy-done.4
  180.3 1.6 fusion.1
  181.9 1.4 convolution_convert_fusion.2
  184.0 1.4 convolution_convert_fusion.1
  185.3 1.4 convolution_convert_fusion
  186.7 2.9 pad_maximum_fusion.1
  190.6 5.6 %fusion.13 = f32[7,8,128,256]{3,2,1,0:T(8,128)} fusion(bf16[7,8,128,128]{3,2,1,0:T(8,128)(2,1)} %bitcast.110, bf16[256,7,128,1]{0,2,3,1:T(8,128)(2,1)S(1)} %get-tuple-element.23), kind=kOutput, calls=%fused_computation.51 | convolution fusion | flops 469762048 | bytes 9633792 | tf_op jit(solution)/shard_map/tfi,fkri->tfkr/dot_general | solution.py:64
  196.2 8.4 %copy.64 = f32[256,56,128]{2,0,1:T(8,128)} copy(f32[256,56,128]{0,2,1:T(8,128)} %bitcast.98) | data formatting | bytes 14680064 | tf_op jit(solution)/shard_map/reshape | solution.py:16
  204.6 5.6 %fusion.4 = f32[7,8,128,256]{3,2,1,0:T(8,128)} fusion(bf16[7,8,128,128]{3,2,1,0:T(8,128)(2,1)} %bitcast.114, bf16[256,7,128]{0,2,1:T(8,128)(2,1)S(1)} %get-tuple-element.22), kind=kOutput, calls=%fused_computation.27 | convolution fusion | flops 469762048 | bytes 9633792 | tf_op jit(solution)/shard_map/tfi,fkri->tfkr/dot_general | solution.py:61
  210.2 8.4 %copy.62 = f32[256,56,128]{2,0,1:T(8,128)} copy(f32[256,56,128]{0,2,1:T(8,128)} %bitcast.99) | data formatting | bytes 14680064 | tf_op jit(solution)/shard_map/reshape | solution.py:16
  218.6 4.3 broadcast.57.clone.1
  222.8 19.0 %scatter_fusion.2 = f32[256,64,128]{2,0,1:T(8,128)} fusion(f32[256,64,128]{2,0,1:T(8,128)} %broadcast.57.clone.1, s32[56]{0:T(128)S(1)} %fusion.8, f32[56,256,128]{2,1,0:T(8,128)} %bitcast.101), kind=kCustom, calls=%fused_computation.5 | custom fusion | flops 1835008 | bytes 22020320 | tf_op jit(solution)/shard_map/scatter-add | solution.py:16
  241.8 4.2 broadcast.57.clone
  246.1 19.1 %scatter_fusion.1 = f32[256,64,128]{2,0,1:T(8,128)} fusion(f32[256,64,128]{2,0,1:T(8,128)} %broadcast.57.clone, s32[56]{0:T(128)S(1)} %fusion.7, f32[56,256,128]{2,1,0:T(8,128)} %bitcast.102), kind=kCustom, calls=%fused_computation.4 | custom fusion | flops 1835008 | bytes 22020320 | tf_op jit(solution)/shard_map/scatter-add | solution.py:16
  265.2 9.5 %add_convert_fusion = bf16[256,64,128]{2,0,1:T(8,128)(2,1)} fusion(f32[256,64,128]{2,0,1:T(8,128)} %scatter_fusion.1, f32[256,64,128]{2,0,1:T(8,128)} %scatter_fusion.2), kind=kLoop, calls=%fused_computation.7 | loop fusion | flops 4194304 | bytes 20971520 | tf_op jit(solution)/shard_map/convert.8
  274.7 6.4 %copy.65 = bf16[256,64,128]{0,2,1:T(8,128)(2,1)} copy(bf16[256,64,128]{2,0,1:T(8,128)(2,1)} %add_convert_fusion) | data formatting | bytes 8388608 | tf_op jit(solution)/shard_map/convert.8
  281.1 4.0 fusion.12
  285.2 8.3 %copy.57 = f32[256,56,128]{2,0,1:T(8,128)} copy(f32[256,56,128]{0,2,1:T(8,128)} %bitcast.100) | data formatting | bytes 14680064 | tf_op jit(solution)/shard_map/reshape | solution.py:16
  293.5 4.2 broadcast.57.clone.2
  297.7 18.8 %scatter_fusion = f32[256,64,128]{2,0,1:T(8,128)} fusion(f32[256,64,128]{2,0,1:T(8,128)} %broadcast.57.clone.2, s32[56]{0:T(128)S(1)} %fusion.6, f32[56,256,128]{2,1,0:T(8,128)} %bitcast.103), kind=kCustom, calls=%fused_computation.3 | custom fusion | flops 1835008 | bytes 22020320 | tf_op jit(solution)/shard_map/scatter-add | solution.py:16
  316.6 6.1 %convert.20 = bf16[256,64,128]{2,0,1:T(8,128)(2,1)} convert(f32[256,64,128]{2,0,1:T(8,128)} %scatter_fusion) | non-fusion elementwise | flops 2097152 | bytes 12582912 | tf_op jit(solution)/shard_map/convert.9
  322.7 6.4 %copy.58 = bf16[256,64,128]{0,2,1:T(8,128)(2,1)} copy(bf16[256,64,128]{2,0,1:T(8,128)(2,1)} %convert.20) | data formatting | bytes 8388608 | tf_op jit(solution)/shard_map/convert.9
  329.0 7.4 %pad_maximum_fusion = bf16[2,256,8192]{1,2,0:T(8,128)(2,1)} fusion(bf16[1,256,8192]{1,2,0:T(8,128)(2,1)} %bitcast.104, bf16[1,256,8192]{1,2,0:T(8,128)(2,1)} %bitcast.107), kind=kLoop, calls=%fused_computation.6 | loop fusion | flops 4194304 | bytes 16777216 | tf_op jit(solution)/shard_map/stack | solution.py:82
  336.5 1.7 fusion.11
  338.3 88.4 %reduce-scatter.3.cloned.1.call-done = bf16[2,256,512]{1,2,0:T(8,128)(2,1)} async-done(((bf16[2,256,8192]{1,2,0:T(8,128)(2,1)}), bf16[2,256,512]{1,2,0:T(8,128)(2,1)}) %reduce-scatter.3.cloned.1.call-update) | async-done | bytes 524304 | tf_op jit(solution)/shard_map/reduce_scatter | solution.py:81
  426.7 1.1 slice_bitcast_fusion
  427.7 0.8 copy.72
  428.6 0.8 copy.73
  (42 shorter events, 2.6 us)
Async XLA Ops:
  7.2 5.8 %copy-start.8 = (s32[7,8]{1,0:T(8,128)S(1)}, s32[7,8]{1,0:T(8,128)}, u32[]{:S(2)}) copy-start(s32[7,8]{1,0:T(8,128)} %param.17) | copy-start | bytes 676
  7.2 5.9 %copy-start.7 = (s32[7,8]{1,0:T(8,128)S(1)}, s32[7,8]{1,0:T(8,128)}, u32[]{:S(2)}) copy-start(s32[7,8]{1,0:T(8,128)} %param.15) | copy-start | bytes 676
  7.2 49.9 %all-gather.3.cloned.1.call-start = ((), (), s32[]{:S(2)}) async-start(), calls=%async_computation.2 | async-start | bytes 5849088 | tf_op jit(solution)/shard_map/all_gather | solution.py:25
  9.0 124.7 %all-gather.5.cloned.1.call-start = ((), (), s32[]{:S(2)}) async-start(), calls=%async_computation.3 | async-start | bytes 8912896 | tf_op jit(solution)/shard_map/all_gather | solution.py:21
  12.1 324.4 %reduce-scatter.5.cloned.1.call-start = ((), (), s32[]{:S(2)}) async-start(), calls=%async_computation.5 | async-start | bytes 5849088 | tf_op jit(solution)/shard_map/reduce_scatter | solution.py:75
  162.4 4.4 %copy-start.2 = (bf16[7,1024,128]{2,1,0:T(8,128)(2,1)S(1)}, bf16[7,1024,128]{2,1,0:T(8,128)(2,1)}, u32[]{:S(2)}) copy-start(bf16[7,1024,128]{2,1,0:T(8,128)(2,1)} %get-tuple-element.18) | copy-start | bytes 5505028
  164.9 1.8 copy-start
  176.5 2.0 copy-start.3
  178.6 1.5 copy-start.4
  178.6 1.7 copy-start.5
  181.9 2.0 copy-start.1
  189.6 0.7 copy-start.6
  189.6 237.0 %reduce-scatter.3.cloned.1.call-start = ((), (), s32[]{:S(2)}) async-start(), calls=%async_computation.4 | async-start | bytes 8912896 | tf_op jit(solution)/shard_map/reduce_scatter | solution.py:81
Sparse Core Ops, SparseCore 0:
  9.9 47.1 all-gather.2
  59.6 74.1 all-gather.4
  189.8 64.9 reduce-scatter.4
  336.6 89.9 reduce-scatter.2
where the time goes:
time: 438 us; the launch traced here: 436 us
  waiting for transfers between devices  204 us (47%)
  local copies, waits for them, and re-layouts  102 us (23%)
  other arithmetic  91 us (21%)
  matrix products  24.6 us (6%)
  between operations  14 us (3%)
    reduce_scatter x1, waiting for transfers between devices, shards(): lax.psum_scatter(jnp.stack([partial_out, partial_in]).astype(jnp.bfloat16...  88.4 us
    all_gather x1, waiting for transfers between devices, shards(): lax.all_gather(jnp.stack([tokens, out_grad]), 'col', axis=2, tiled=True)  71.8 us
    scatter-add x3, other arithmetic, spread(): zero_block.at[:, block_lists.reshape(-1)]  56.9 us
    all_gather x1, waiting for transfers between devices, shards(): lax.all_gather(jnp.concatenate([gate_weight, up_weight, down_weight], axi...  43.8 us
    another operation x5, local copies, waits for them, and re-layouts  25.5 us
    reshape x3, local copies, waits for them, and re-layouts, spread(): contrib.reshape(rows_here, -1, BS)  25.1 us
    another operation x2, other arithmetic  15.6 us
  transfers between devices with their start and end apart: 4, of which 3 were waited for; matrix products, arithmetic and copies ran while one was open for 36% of the time, Pallas kernels for 0%

commit v1 on v0

--- a/solution.py
+++ b/solution.py
@@ -8,6 +8,11 @@
 KG = 8
 KH = 8
 DB = 64
+
+
+def exchange_gather(block, name, along):
+    outgoing = jnp.stack([block] * lax.axis_size(name))
+    return jnp.concatenate(lax.all_to_all(outgoing, name, 0, 0), axis=along)
 
 
 def spread(contrib, block_lists):
@@ -22,8 +27,8 @@
     panel_in, panel_grad = (panels[0], panels[1])
     rows_here = panel_in.shape[0]
     owned_slots = gate_weight.shape[0]
-    tiles = lax.all_gather(
-        jnp.concatenate([gate_weight, up_weight, down_weight], axis=0), "row", axis=1, tiled=True
+    tiles = exchange_gather(
+        jnp.concatenate([gate_weight, up_weight, down_weight], axis=0), "row", 1
     )
     gate_tiles = tiles[:owned_slots]
     up_tiles = tiles[owned_slots : 2 * owned_slots]

time: 438 us -> 456 us (1.041)
  starting transfers between devices: 0.34 us -> 8.87 us
  waiting for transfers between devices: 204 us -> 210 us
  local copies, waits for them, and re-layouts: 102 us -> 107 us
    all_to_all x0 -> x1, waiting for transfers between devices: none -> 122 us  [exchange_gather(): return jnp.concatenate(lax.all_to_all(outgoing, name, 0, 0), axis=along)]
    all_gather x1, waiting for transfers between devices: 71.8 us -> 0.01 us  [shards(): lax.all_gather(jnp.stack([tokens, out_grad]), 'col', axis=2, tiled=True)]
    all_gather x1 -> x0, waiting for transfers between devices: 43.8 us -> none  [shards(): lax.all_gather(jnp.concatenate([gate_weight, up_weight, down_weight], axi...]
    all_to_all x0 -> x1, starting transfers between devices: none -> 8.75 us  [exchange_gather(): return jnp.concatenate(lax.all_to_all(outgoing, name, 0, 0), axis=along)]
    another operation x5 -> x6, local copies, waits for them, and re-layouts: 25.5 us -> 29.3 us
  transfers between devices with their start and end apart: 4 -> 4, of which waited for: 3 -> 2; matrix products, arithmetic and copies ran while one was open for 36% -> 35% of each run, Pallas kernels for 0% -> 0%
where the time goes in v1:
time: 456 us; the launch traced here: 454 us
  waiting for transfers between devices  210 us (46%)
  local copies, waits for them, and re-layouts  107 us (23%)
  other arithmetic  90.4 us (20%)
  matrix products  24.6 us (5%)
  between operations  14 us (3%)
  starting transfers between devices  8.87 us (2%)
    all_to_all x1, waiting for transfers between devices, exchange_gather(): return jnp.concatenate(lax.all_to_all(outgoing, name, 0, 0), axis=along)  122 us
    reduce_scatter x1, waiting for transfers between devices, shards(): lax.psum_scatter(jnp.stack([partial_out, partial_in]).astype(jnp.bfloat16...  87.7 us
    scatter-add x3, other arithmetic, spread(): zero_block.at[:, block_lists.reshape(-1)]  57.1 us
    another operation x5, local copies, waits for them, and re-layouts  25.6 us
    reshape x3, local copies, waits for them, and re-layouts, spread(): contrib.reshape(rows_here, -1, BS)  25.1 us
    another operation x2, other arithmetic  15.6 us
  transfers between devices with their start and end apart: 4, of which 2 were waited for; matrix products, arithmetic and copies ran while one was open for 35% of the time, Pallas kernels for 0%

profile of v1, /device:TPU:2, one launch (start us, length us, event | category | flops | bytes accessed | tf_op | source)
XLA Modules:
  0.0 454.4 jit_solution(12689034781573418431)
XLA Ops:
  7.2 1.1 copy.75
  8.3 1.1 copy.76
  9.4 0.8 pad_maximum_fusion.2
  10.2 1.1 pad_maximum_fusion.3
  11.3 3.8 stack.11
  15.1 8.7 %all-to-all-start = ((bf16[16,21,64,128]{3,2,1,0:T(8,128)(2,1)}), bf16[16,21,64,128]{3,2,1,0:T(8,128)(2,1)}, u32[]{:S(2)}, u32[]{:S(2)}) async-start(bf16[16,21,64,128]{3,2,1,0:T(8,128)(2,1)} %stack.11), calls=%async_computation | async-start | bytes 11010048 | tf_op jit(solution)/shard_map/all_to_all | solution.py:15
  24.3 122.0 %all-to-all-done = bf16[16,21,64,128]{3,2,1,0:T(8,128)(2,1)} async-done(((bf16[16,21,64,128]{3,2,1,0:T(8,128)(2,1)}), bf16[16,21,64,128]{3,2,1,0:T(8,128)(2,1)}, u32[]{:S(2)}, u32[]{:S(2)}) %all-to-all-start) | async-done | bytes 5505056 | tf_op jit(solution)/shard_map/all_to_all | solution.py:15
  146.3 3.9 copy.127
  150.2 3.1 fusion.10
  153.3 5.7 %fusion.9 = (bf16[1,256,8192]{1,2,0:T(8,128)(2,1)}, bf16[1,256,8192]{1,2,0:T(8,128)(2,1)}) fusion(bf16[2,256,8192]{1,2,0:T(8,128)(2,1)} %all-gather.2.cloned.1.call-done), kind=kLoop, calls=%fused_computation.48 | loop fusion | bytes 16777216 | tf_op jit(solution)/shard_map/slice | solution.py:27
  159.0 6.4 %copy.77 = bf16[256,64,128]{2,0,1:T(8,128)(2,1)} copy(bf16[256,64,128]{0,2,1:T(8,128)(2,1)} %bitcast.110) | data formatting | bytes 8388608 | tf_op jit(solution)/shard_map/reshape;squeeze | solution.py:38
  165.4 6.4 %copy.84 = bf16[256,64,128]{2,0,1:T(8,128)(2,1)} copy(bf16[256,64,128]{0,2,1:T(8,128)(2,1)} %bitcast.109) | data formatting | bytes 8388608 | tf_op jit(solution)/shard_map/reshape;squeeze | solution.py:55
  171.7 5.1 %gather_fusion.1 = bf16[56,256,128]{2,1,0:T(8,128)(2,1)} fusion(bf16[256,64,128]{2,0,1:T(8,128)(2,1)} %copy.77, s32[1024]{0:T(1024)S(1)} %pad_clamp_fusion.1), kind=kCustom, calls=%fused_computation.1.clone | custom fusion | bytes 7340256 | tf_op jit(solution)/shard_map/jit(_take)/gather | solution.py:42
  176.8 5.1 %gather_fusion = bf16[56,256,128]{2,1,0:T(8,128)(2,1)} fusion(bf16[256,64,128]{2,0,1:T(8,128)(2,1)} %copy.77, s32[1024]{0:T(1024)S(1)} %pad_clamp_fusion.2), kind=kCustom, calls=%fused_computation.clone | custom fusion | bytes 7340256 | tf_op jit(solution)/shard_map/jit(_take)/gather | solution.py:39
  181.9 2.6 broadcast_select_fusion.1
  184.5 1.8 copy-done
  186.3 2.3 convolution_bitcast_fusion.1
  188.6 5.1 %gather_fusion.2 = bf16[56,256,128]{2,1,0:T(8,128)(2,1)} fusion(bf16[256,64,128]{2,0,1:T(8,128)(2,1)} %copy.84, s32[1024]{0:T(1024)S(1)} %pad_clamp_fusion), kind=kCustom, calls=%fused_computation.2.clone | custom fusion | bytes 7340256 | tf_op jit(solution)/shard_map/jit(_take)/gather | solution.py:56
  193.7 2.4 broadcast_select_fusion
  196.1 1.4 convolution_bitcast_fusion
  198.6 1.1 copy-done.4
  199.9 1.6 fusion.1
  201.5 1.4 convolution_convert_fusion.2
  203.5 1.4 convolution_convert_fusion.1
  204.9 1.4 convolution_convert_fusion
  206.2 2.9 pad_maximum_fusion.1
  209.5 5.6 %fusion.13 = f32[7,8,128,256]{3,2,1,0:T(8,128)} fusion(bf16[7,8,128,128]{3,2,1,0:T(8,128)(2,1)} %bitcast.114, bf16[256,7,128,1]{0,2,3,1:T(8,128)(2,1)S(1)} %get-tuple-element.28), kind=kOutput, calls=%fused_computation.52 | convolution fusion | flops 469762048 | bytes 9633792 | tf_op jit(solution)/shard_map/tfi,fkri->tfkr/dot_general | solution.py:69
  215.1 8.4 %copy.89 = f32[256,56,128]{2,0,1:T(8,128)} copy(f32[256,56,128]{0,2,1:T(8,128)} %bitcast.101) | data formatting | bytes 14680064 | tf_op jit(solution)/shard_map/reshape | solution.py:21
  223.5 5.6 %fusion.4 = f32[7,8,128,256]{3,2,1,0:T(8,128)} fusion(bf16[7,8,128,128]{3,2,1,0:T(8,128)(2,1)} %bitcast.118, bf16[256,7,128]{0,2,1:T(8,128)(2,1)S(1)} %get-tuple-element.27), kind=kOutput, calls=%fused_computation.28 | convolution fusion | flops 469762048 | bytes 9633792 | tf_op jit(solution)/shard_map/tfi,fkri->tfkr/dot_general | solution.py:66
  229.1 8.4 %copy.87 = f32[256,56,128]{2,0,1:T(8,128)} copy(f32[256,56,128]{0,2,1:T(8,128)} %bitcast.102) | data formatting | bytes 14680064 | tf_op jit(solution)/shard_map/reshape | solution.py:21
  237.5 4.3 broadcast.59.clone.1
  241.7 19.1 %scatter_fusion.2 = f32[256,64,128]{2,0,1:T(8,128)} fusion(f32[256,64,128]{2,0,1:T(8,128)} %broadcast.59.clone.1, s32[56]{0:T(128)S(1)} %fusion.8, f32[56,256,128]{2,1,0:T(8,128)} %bitcast.104), kind=kCustom, calls=%fused_computation.5 | custom fusion | flops 1835008 | bytes 22020320 | tf_op jit(solution)/shard_map/scatter-add | solution.py:21
  260.8 4.3 broadcast.59.clone
  265.1 19.1 %scatter_fusion.1 = f32[256,64,128]{2,0,1:T(8,128)} fusion(f32[256,64,128]{2,0,1:T(8,128)} %broadcast.59.clone, s32[56]{0:T(128)S(1)} %fusion.7, f32[56,256,128]{2,1,0:T(8,128)} %bitcast.105), kind=kCustom, calls=%fused_computation.4 | custom fusion | flops 1835008 | bytes 22020320 | tf_op jit(solution)/shard_map/scatter-add | solution.py:21
  284.2 9.5 %add_convert_fusion = bf16[256,64,128]{2,0,1:T(8,128)(2,1)} fusion(f32[256,64,128]{2,0,1:T(8,128)} %scatter_fusion.1, f32[256,64,128]{2,0,1:T(8,128)} %scatter_fusion.2), kind=kLoop, calls=%fused_computation.7 | loop fusion | flops 4194304 | bytes 20971520 | tf_op jit(solution)/shard_map/convert.8
  293.7 6.4 %copy.90 = bf16[256,64,128]{0,2,1:T(8,128)(2,1)} copy(bf16[256,64,128]{2,0,1:T(8,128)(2,1)} %add_convert_fusion) | data formatting | bytes 8388608 | tf_op jit(solution)/shard_map/convert.8
  300.1 4.0 fusion.12
  304.2 8.3 %copy.82 = f32[256,56,128]{2,0,1:T(8,128)} copy(f32[256,56,128]{0,2,1:T(8,128)} %bitcast.103) | data formatting | bytes 14680064 | tf_op jit(solution)/shard_map/reshape | solution.py:21
  312.5 4.3 broadcast.59.clone.2
  316.8 18.9 %scatter_fusion = f32[256,64,128]{2,0,1:T(8,128)} fusion(f32[256,64,128]{2,0,1:T(8,128)} %broadcast.59.clone.2, s32[56]{0:T(128)S(1)} %fusion.6, f32[56,256,128]{2,1,0:T(8,128)} %bitcast.106), kind=kCustom, calls=%fused_computation.3 | custom fusion | flops 1835008 | bytes 22020320 | tf_op jit(solution)/shard_map/scatter-add | solution.py:21
  335.7 6.1 %convert.20 = bf16[256,64,128]{2,0,1:T(8,128)(2,1)} convert(f32[256,64,128]{2,0,1:T(8,128)} %scatter_fusion) | non-fusion elementwise | flops 2097152 | bytes 12582912 | tf_op jit(solution)/shard_map/convert.9
  341.8 6.4 %copy.83 = bf16[256,64,128]{0,2,1:T(8,128)(2,1)} copy(bf16[256,64,128]{2,0,1:T(8,128)(2,1)} %convert.20) | data formatting | bytes 8388608 | tf_op jit(solution)/shard_map/convert.9
  348.1 7.5 %pad_maximum_fusion = bf16[2,256,8192]{1,2,0:T(8,128)(2,1)} fusion(bf16[1,256,8192]{1,2,0:T(8,128)(2,1)} %bitcast.108, bf16[1,256,8192]{1,2,0:T(8,128)(2,1)} %bitcast.111), kind=kLoop, calls=%fused_computation.6 | loop fusion | flops 4194304 | bytes 16777216 | tf_op jit(solution)/shard_map/stack | solution.py:87
  355.7 1.7 fusion.11
  357.4 87.7 %reduce-scatter.3.cloned.1.call-done = bf16[2,256,512]{1,2,0:T(8,128)(2,1)} async-done(((bf16[2,256,8192]{1,2,0:T(8,128)(2,1)}), bf16[2,256,512]{1,2,0:T(8,128)(2,1)}) %reduce-scatter.3.cloned.1.call-update) | async-done | bytes 524304 | tf_op jit(solution)/shard_map/reduce_scatter | solution.py:86
  445.1 1.1 slice_bitcast_fusion
  446.2 0.8 copy.97
  447.0 0.8 copy.98
  (43 shorter events, 2.7 us)
Async XLA Ops:
  7.2 146.1 %all-gather.2.cloned.1.call-start = ((), (), s32[]{:S(2)}) async-start(), calls=%async_computation.3 | async-start | bytes 8912896 | tf_op jit(solution)/shard_map/all_gather | solution.py:26
  15.1 8.8 %copy-start.6 = (s32[7,8]{1,0:T(8,128)S(1)}, s32[7,8]{1,0:T(8,128)}, u32[]{:S(2)}) copy-start(s32[7,8]{1,0:T(8,128)} %param.16) | copy-start | bytes 676
  15.1 8.9 %copy-start.8 = (s32[7,8]{1,0:T(8,128)S(1)}, s32[7,8]{1,0:T(8,128)}, u32[]{:S(2)}) copy-start(s32[7,8]{1,0:T(8,128)} %param.17) | copy-start | bytes 676
  15.1 9.0 %copy-start.7 = (s32[7,8]{1,0:T(8,128)S(1)}, s32[7,8]{1,0:T(8,128)}, u32[]{:S(2)}) copy-start(s32[7,8]{1,0:T(8,128)} %param.15) | copy-start | bytes 676
  15.1 131.2 %all-to-all-start = ((bf16[16,21,64,128]{3,2,1,0:T(8,128)(2,1)}), bf16[16,21,64,128]{3,2,1,0:T(8,128)(2,1)}, u32[]{:S(2)}, u32[]{:S(2)}) async-start(bf16[16,21,64,128]{3,2,1,0:T(8,128)(2,1)} %stack.11), calls=%async_computation | async-start | bytes 11010048 | tf_op jit(solution)/shard_map/all_to_all | solution.py:15
  23.8 331.8 %reduce-scatter.5.cloned.1.call-start = ((), (), s32[]{:S(2)}) async-start(), calls=%async_computation.5 | async-start | bytes 5849088 | tf_op jit(solution)/shard_map/reduce_scatter | solution.py:80
  181.9 4.4 copy-start.2
  184.5 1.8 copy-start
  196.1 2.0 copy-start.3
  198.1 1.5 copy-start.4
  198.1 1.7 copy-start.5
  201.5 2.0 copy-start.1
  209.2 235.9 %reduce-scatter.3.cloned.1.call-start = ((), (), s32[]{:S(2)}) async-start(), calls=%async_computation.4 | async-start | bytes 8912896 | tf_op jit(solution)/shard_map/reduce_scatter | solution.py:86
Sparse Core Ops, SparseCore 0:
  10.5 78.7 all-gather.1
  209.3 64.2 reduce-scatter.4
  355.7 89.2 reduce-scatter.2
